TPU v7x, 32 devices: a whole 2x2x4 slice. The times are simulated.
32 devices in a mesh: dp: 8 (over y, x, core), tensor: 4 (over z).
Axes of the slice: x: 2, y: 2, z: 4, core: 2. Of those that a mesh axis runs over, the one named last changes fastest.
Arguments:
- hidden_in: bfloat16 [32, 512, 768], P('dp'), may hold values from -6 to 6
- out_grad: bfloat16 [32, 512, 768], P('dp'), may hold values from -3 to 3
- segment_ids: int32 [32, 512], P('dp'), may hold values from 0 to 7, never falling along the last dimension, each value on 1 to 256 neighbouring positions
- step_count: int32 [1], replicated, may hold values from 1 to 199999
- qkv_state: float32 [3, 768, 3, 768], P(None, 'dp', None, 'tensor'), as said below
- qv_bias_state: float32 [3, 2, 12, 64], P(None, None, 'tensor', 'dp'), as said below
- out_state: float32 [3, 768, 768], P(None, 'tensor', 'dp'), as said below
- up_state: float32 [3, 768, 3072], P(None, 'dp', 'tensor'), as said below
- up_bias_state: float32 [3, 24, 128], P(None, 'tensor', 'dp'), as said below
- down_state: float32 [3, 3072, 768], P(None, 'tensor', 'dp'), as said below
- vector_state: float32 [3, 6, 768], P(None, None, 'dp'), as said below
Outputs:
- hidden_out: bfloat16 [32, 512, 768], P('dp')
- grad_in: bfloat16 [32, 512, 768], P('dp')
- grad_qkv: float32 [768, 3, 768], P('dp', None, 'tensor')
- grad_qv_bias: float32 [2, 12, 64], P(None, 'tensor', 'dp')
- grad_out: float32 [768, 768], P('tensor', 'dp')
- grad_up: float32 [768, 3072], P('dp', 'tensor')
- grad_up_bias: float32 [24, 128], P('tensor', 'dp')
- grad_down: float32 [3072, 768], P('tensor', 'dp')
- grad_vectors: float32 [6, 768], P(None, 'dp')
- new_qkv_state: float32 [2, 768, 3, 768], P(None, 'dp', None, 'tensor')
- new_qv_bias_state: float32 [2, 2, 12, 64], P(None, None, 'tensor', 'dp')
- new_out_state: float32 [2, 768, 768], P(None, 'tensor', 'dp')
- new_up_state: float32 [2, 768, 3072], P(None, 'dp', 'tensor')
- new_up_bias_state: float32 [2, 24, 128], P(None, 'tensor', 'dp')
- new_down_state: float32 [2, 3072, 768], P(None, 'tensor', 'dp')
- new_vector_state: float32 [2, 6, 768], P(None, None, 'dp')
- plan: float32 [3], replicated
Inputs may be any that keep to these rules, and one draw needn't show every extreme that they name: `segment_ids`: within each packed row the fragment numbers never fall; a token attends exactly to the tokens of its own row with the same number. `qkv_state`: index 2 (second moments) is positive. `qv_bias_state`: index 2 (second moments) is positive. `out_state`: index 2 (second moments) is positive. `up_state`: index 2 (second moments) is positive. `up_bias_state`: index 2 (second moments) is positive. `down_state`: index 2 (second moments) is positive. `vector_state`: index 2 (second moments) is positive.
All inputs are finite; a program needn't handle non-finite values.
Results may differ from a plain program's by a relative error of at most 0.023.
The roundings to bfloat16 on the way count: a program that leaves them out, or rounds other values in their place, can miss the bound.
Values may be sent and summed in bfloat16 or wider, within the bound.
No kernel may reach another device: no remote copies, remote signals or barrier semaphores. Data moves between devices by JAX's collectives and lax.ppermute only.
A program may use at most 192 MiB of HBM per device.

v0:
```python
import math
import jax
import jax.numpy as jnp
from jax import lax
from jax.sharding import PartitionSpec as P

HD = 64
norm_eps = 1e-05
beta_first = 0.9
beta_second = 0.999
warm_steps = 10000.0
total_steps = 200000.0


def layer_norm(value, gain, shift):
    center = value - jnp.mean(value, axis=-1, keepdims=True)
    spread = jnp.mean(center * center, axis=-1, keepdims=True)
    return center * lax.rsqrt(spread + norm_eps) * gain + shift


def gelu_exact(value):
    return 0.5 * value * (1.0 + lax.erf(value * 0.7071067811865476))


def scores_of(query, key_rows, segments):
    raw = jnp.einsum(
        "bqhd,bkhd->bhqk", query, key_rows, preferred_element_type=jnp.float32
    ) * HD ** (-0.5)
    same = segments[:, :, None] == segments[:, None, :]
    return jnp.where(same[:, None], raw, -1e30)


def contract_rows(left, right):
    return lax.dot_general(
        left, right, (((0,), (0,)), ((), ())), preferred_element_type=jnp.float32
    )


def contract_cols(left, right):
    return lax.dot_general(
        left, right, (((1,), (1,)), ((), ())), preferred_element_type=jnp.float32
    )


def moment_update(state, grad):
    moment_one = beta_first * state[1] + (1.0 - beta_first) * grad
    moment_two = beta_second * state[2] + (1.0 - beta_second) * grad * grad
    return jnp.stack([moment_one, moment_two])


def body(
    hidden_in,
    out_grad,
    segment_ids,
    step_count,
    qkv_state,
    qv_bias_state,
    out_state,
    up_state,
    up_bias_state,
    down_state,
    vector_state,
):
    bf = jnp.bfloat16
    fl = jnp.float32
    w_qkv, b_qv, w_out, w_up, b_up, w_down, vectors = (
        lax.all_gather(qkv_state[0].astype(bf), "dp", axis=0, tiled=True),
        lax.all_gather(qv_bias_state[0].astype(bf), "dp", axis=2, tiled=True),
        lax.all_gather(out_state[0].astype(bf), "dp", axis=1, tiled=True),
        lax.all_gather(up_state[0].astype(bf), "dp", axis=0, tiled=True),
        lax.all_gather(up_bias_state[0].astype(bf), "dp", axis=1, tiled=True),
        lax.all_gather(down_state[0].astype(bf), "dp", axis=1, tiled=True),
        lax.all_gather(vector_state[0].astype(bf), "dp", axis=1, tiled=True),
    )
    count, length, width_model = hidden_in.shape
    rows = count * length
    heads_local = b_qv.shape[1]
    head_width = heads_local * HD
    ff_local = w_up.shape[1]
    scale = HD ** (-0.5)
    plain = hidden_in.reshape(rows, width_model)
    cotangent = out_grad.reshape(rows, width_model)
    vec = vectors.astype(fl)
    proj = jnp.einsum("td,dcf->tcf", plain, w_qkv, preferred_element_type=fl)
    bias_f = b_qv.astype(fl).reshape(2, head_width)
    bias = jnp.stack([bias_f[0], jnp.zeros((head_width,), fl), bias_f[1]])
    proj_b = (proj + bias[None]).astype(bf)
    heads = proj_b.reshape(count, length, 3, heads_local, HD)
    query = heads[:, :, 0]
    key_rows = heads[:, :, 1]
    value_rows = heads[:, :, 2]
    scores = scores_of(query, key_rows, segment_ids)
    top = jnp.max(scores, axis=-1, keepdims=True)
    expd = jnp.exp(scores - top)
    denom = jnp.sum(expd, axis=-1, keepdims=True)
    log_total = top + jnp.log(denom)
    probs_b = (expd / denom).astype(bf)
    context = (
        jnp.einsum("bhqk,bkhd->bqhd", probs_b, value_rows, preferred_element_type=fl)
        .astype(bf)
        .reshape(rows, head_width)
    )
    attn_part = jnp.dot(context, w_out, preferred_element_type=fl)
    attn = lax.psum(attn_part.astype(jnp.bfloat16), "tensor").astype(jnp.float32)
    first, first_pull = jax.vjp(layer_norm, plain.astype(fl) + attn + vec[4], vec[0], vec[1])
    first_b = first.astype(bf)
    up = jnp.dot(first_b, w_up, preferred_element_type=fl) + b_up.astype(fl).reshape(ff_local)
    act, gelu_pull = jax.vjp(gelu_exact, up)
    act_b = act.astype(bf)
    ffn_part = jnp.dot(act_b, w_down, preferred_element_type=fl)
    ffn = lax.psum(ffn_part.astype(jnp.bfloat16), "tensor").astype(jnp.float32)
    out, second_pull = jax.vjp(layer_norm, first + ffn + vec[5], vec[2], vec[3])
    grad_r2, grad_g2, grad_b2 = second_pull(cotangent.astype(fl))
    grad_ffn = grad_r2.astype(bf)
    grad_down = contract_rows(act_b, grad_ffn)
    grad_act = contract_cols(grad_ffn, w_down)
    grad_up_b = gelu_pull(grad_act)[0].astype(bf)
    grad_wup = contract_rows(first_b, grad_up_b)
    grad_bup = jnp.sum(grad_up_b, axis=0, dtype=fl).reshape(b_up.shape)
    feed_part = contract_cols(grad_up_b, w_up)
    feed_back = lax.psum(feed_part.astype(jnp.bfloat16), "tensor").astype(jnp.float32)
    grad_first = grad_r2 + feed_back.astype(bf).astype(fl)
    grad_r1, grad_g1, grad_b1 = first_pull(grad_first)
    grad_attn = grad_r1.astype(bf)
    grad_wout = contract_rows(context, grad_attn)
    grad_context = (
        contract_cols(grad_attn, w_out).astype(bf).reshape(count, length, heads_local, HD)
    )
    again = scores_of(query, key_rows, segment_ids)
    probs = jnp.exp(again - log_total)
    probs_again = probs.astype(bf)
    grad_probs = jnp.einsum("bqhd,bkhd->bhqk", grad_context, value_rows, preferred_element_type=fl)
    grad_value = jnp.einsum("bhqk,bqhd->bkhd", probs_again, grad_context, preferred_element_type=fl)
    row_dot = jnp.sum(probs * grad_probs, axis=-1, keepdims=True)
    grad_scores = (probs * (grad_probs - row_dot)).astype(bf)
    grad_query = (
        jnp.einsum("bhqk,bkhd->bqhd", grad_scores, key_rows, preferred_element_type=fl) * scale
    )
    grad_key = jnp.einsum("bhqk,bqhd->bkhd", grad_scores, query, preferred_element_type=fl) * scale
    grad_proj = (
        jnp.stack([grad_query, grad_key, grad_value], axis=2)
        .astype(bf)
        .reshape(rows, 3, head_width)
    )
    proj_sums = jnp.sum(grad_proj, axis=0, dtype=fl)
    grad_bqv = jnp.stack([proj_sums[0], proj_sums[2]]).reshape(2, heads_local, HD)
    grad_wqkv = jnp.einsum("td,tcf->dcf", plain, grad_proj, preferred_element_type=fl)
    input_part = jnp.einsum("tcf,dcf->td", grad_proj, w_qkv, preferred_element_type=fl)
    vec_part = jnp.stack(
        [grad_g1, grad_b1, grad_g2, grad_b2, jnp.sum(grad_r1, axis=0), jnp.sum(grad_r2, axis=0)]
    )
    input_back = lax.psum(input_part.astype(jnp.bfloat16), "tensor").astype(jnp.float32)
    grad_in = (grad_r1 + input_back.astype(bf).astype(fl)).astype(bf).reshape(hidden_in.shape)
    hidden_out = out.astype(bf).reshape(hidden_in.shape)
    summed = (
        lax.psum_scatter(grad_wqkv, "dp", scatter_dimension=0, tiled=True),
        lax.psum_scatter(grad_bqv, "dp", scatter_dimension=2, tiled=True),
        lax.psum_scatter(grad_wout, "dp", scatter_dimension=1, tiled=True),
        lax.psum_scatter(grad_wup, "dp", scatter_dimension=0, tiled=True),
        lax.psum_scatter(grad_bup, "dp", scatter_dimension=1, tiled=True),
        lax.psum_scatter(grad_down, "dp", scatter_dimension=1, tiled=True),
        lax.psum_scatter(vec_part, "dp", scatter_dimension=1, tiled=True),
    )
    steps_f = step_count[0].astype(fl)
    factor = jnp.minimum(steps_f / warm_steps, (total_steps - steps_f) / (total_steps - warm_steps))
    fix_first = 1.0 - jnp.exp(steps_f * math.log(beta_first))
    fix_second = 1.0 - jnp.exp(steps_f * math.log(beta_second))
    states = (
        qkv_state,
        qv_bias_state,
        out_state,
        up_state,
        up_bias_state,
        down_state,
        vector_state,
    )
    news = tuple((moment_update(s, g) for s, g in zip(states, summed)))
    plan = jnp.stack([factor, fix_first, fix_second])
    return (
        hidden_out,
        grad_in,
        summed[0],
        summed[1],
        summed[2],
        summed[3],
        summed[4],
        summed[5],
        summed[6],
        news[0],
        news[1],
        news[2],
        news[3],
        news[4],
        news[5],
        news[6],
        plan,
    )


def solution(mesh):
    return jax.shard_map(
        body,
        mesh=mesh,
        in_specs=(
            P("dp", None, None),
            P("dp", None, None),
            P("dp", None),
            P(),
            P(None, "dp", None, "tensor"),
            P(None, None, "tensor", "dp"),
            P(None, "tensor", "dp"),
            P(None, "dp", "tensor"),
            P(None, "tensor", "dp"),
            P(None, "tensor", "dp"),
            P(None, None, "dp"),
        ),
        out_specs=(
            P("dp", None, None),
            P("dp", None, None),
            P("dp", None, "tensor"),
            P(None, "tensor", "dp"),
            P("tensor", "dp"),
            P("dp", "tensor"),
            P("tensor", "dp"),
            P("tensor", "dp"),
            P(None, "dp"),
            P(None, "dp", None, "tensor"),
            P(None, None, "tensor", "dp"),
            P(None, "tensor", "dp"),
            P(None, "dp", "tensor"),
            P(None, "tensor", "dp"),
            P(None, "tensor", "dp"),
            P(None, None, "dp"),
            P(),
        ),
        check_vma=False,
    )
```

profile of v0, /device:TPU:0, one launch (start us, length us, event | category | flops | bytes accessed | tf_op | source)
XLA Modules:
  0.0 760.8 jit_solution(6386560561636301362)
XLA Ops:
  9.0 10.6 %all-gather.1 = bf16[1,2,3,64]{2,1,0,3:T(2,128)(2,1)S(1)} all-gather(bf16[1,2,3,8]{2,1,0,3:T(2,128)(2,1)S(1)} %copy.181), channel_id=3, replica_groups=mesh['dp'=8,'tensor'=4] {'dp'}, dimensions={3}, use_global_device_ids=true | all-gather | bytes 864 | tf_op jit(solution)/shard_map/all_gather | solution.py:68
  22.8 11.3 %all-gather.2 = bf16[1,192,768]{1,0,2:T(2,128)(2,1)} all-gather(bf16[1,192,96]{1,0,2:T(2,128)(2,1)S(1)} %copy.142), channel_id=4, replica_groups=mesh['dp'=8,'tensor'=4] {'dp'}, dimensions={2}, use_global_device_ids=true | all-gather | bytes 331776 | tf_op jit(solution)/shard_map/all_gather | solution.py:69
  38.6 15.8 %all-gather = bf16[1,768,3,192]{3,2,0,1:T(4,128)(2,1)} all-gather(bf16[1,96,3,192]{3,2,0,1:T(4,128)(2,1)} %copy.132), channel_id=2, replica_groups=mesh['dp'=8,'tensor'=4] {'dp'}, dimensions={1}, use_global_device_ids=true | all-gather | bytes 995328 | tf_op jit(solution)/shard_map/all_gather | solution.py:67
  62.9 6.2 reshape.215
  71.5 4.4 fusion.73
  93.2 8.7 %all-gather.5 = bf16[1,6,128]{1,0,2:T(2,128)(2,1)S(1)} all-gather(bf16[1,6,16]{1,0,2:T(2,128)(2,1)} %copy.145), channel_id=7, replica_groups=mesh['dp'=8,'tensor'=4] {'dp'}, dimensions={2}, use_global_device_ids=true | all-gather | bytes 1728 | tf_op jit(solution)/shard_map/all_gather | solution.py:71
  103.2 10.8 %all-gather.3 = bf16[1,6,768]{1,0,2:T(2,128)(2,1)S(1)} all-gather(bf16[1,6,96]{1,0,2:T(2,128)(2,1)S(1)} %copy.185), channel_id=5, replica_groups=mesh['dp'=8,'tensor'=4] {'dp'}, dimensions={2}, use_global_device_ids=true | all-gather | bytes 10368 | tf_op jit(solution)/shard_map/all_gather | solution.py:73
  114.4 13.0 %slice_reduce_fusion.1 = (f32[768]{0:T(1024)S(1)}, f32[768]{0:T(1024)S(1)}, f32[768]{0:T(1024)S(1)}, f32[768]{0:T(1024)S(1)}, f32[768]{0:T(1024)S(1)}, /*index=5*/f32[768]{0:T(1024)S(1)}) fusion(f32[1,6,768]{1,0,2:T(1,128)S(1)} %convert_element_type.169), kind=kLoop, calls=%fused_computation.78 | loop fusion | bytes 36864 | tf_op jit(solution)/shard_map/slice | solution.py:112
  127.4 81.6 %all-reduce.6.cloned.1.call-done = bf16[2048,768]{1,0:T(8,128)(2,1)} async-done(((bf16[2048,768]{1,0:T(8,128)(2,1)}), bf16[2048,768]{1,0:T(8,128)(2,1)}) %all-reduce.6.cloned.1.call-update) | async-done | bytes 3145744 | tf_op jit(solution)/shard_map/psum | solution.py:104
  215.8 7.4 multiply_convert_fusion.1
  223.3 6.2 convolution_convert_fusion.1
  229.7 120.0 %all-reduce.8.cloned.1.call-done = bf16[2048,768]{1,0:T(8,128)(2,1)} async-done(((bf16[2048,768]{1,0:T(8,128)(2,1)}), bf16[2048,768]{1,0:T(8,128)(2,1)}) %all-reduce.8.cloned.1.call-update) | async-done | bytes 3145744 | tf_op jit(solution)/shard_map/psum | solution.py:111
  349.7 4.8 fusion.67
  359.5 4.3 fusion.66
  363.8 5.9 convert_reduce_fusion.1
  376.4 8.0 %fusion.60 = f32[768,768]{0,1:T(8,128)} fusion(bf16[2048,768]{1,0:T(8,128)(2,1)} %copy-done.36, f32[2048,768]{1,0:T(8,128)} %copy-done.2, f32[2048]{0:T(1024)S(1)} %negate_multiply_fusion.1), kind=kOutput, calls=%fused_computation.147 | convolution fusion | flops 2419064832 | bytes 11804672 | tf_op jit(solution)/shard_map/dot_general | solution.py:34
  384.5 8.0 %fusion.61 = f32[768,768]{1,0:T(8,128)} fusion(bf16[2048,768]{1,0:T(8,128)(2,1)} %copy-done.35, f32[2048,768]{1,0:T(8,128)} %get-tuple-element.123, f32[768]{0:T(1024)} %copy-done.24, f32[768]{0:T(1024)} %copy-done.22, f32[2048]{0:T(1024)S(1)} %fusion.49), kind=kOutput, calls=%fused_computation.148 | convolution fusion | flops 2422210560 | bytes 11810816 | tf_op jit(solution)/shard_map/dot_general | solution.py:34
  392.8 102.9 %all-reduce.10.cloned.1.call-done = bf16[2048,768]{1,0:T(8,128)(2,1)} async-done(((bf16[2048,768]{1,0:T(8,128)(2,1)}), bf16[2048,768]{1,0:T(8,128)(2,1)}) %all-reduce.10.cloned.1.call-update) | async-done | bytes 3145744 | tf_op jit(solution)/shard_map/psum | solution.py:121
  495.7 8.0 %multiply_reduce_fusion.1 = (f32[768]{0:T(1024)}, f32[2048]{0:T(1024)S(1)}, f32[768]{0:T(1024)}, f32[768]{0:T(1024)}) fusion(f32[2048,768]{1,0:T(8,128)} %get-tuple-element.123, f32[2048]{0:T(1024)S(1)} %fusion.49, bf16[2048,768]{1,0:T(8,128)(2,1)} %all-reduce.10.cloned.1.call-done, f32[2048,768]{1,0:T(8,128)} %copy-done.2, ...), kind=kLoop, calls=%fused_computation.19 | loop fusion | flops 17297152 | bytes 15765504 | tf_op jit(solution)/shard_map/transpose(jvp())/reduce_sum | solution.py:18
  503.7 6.1 fusion.65
  517.6 8.3 %multiply_reduce_fusion = (f32[4,3,512]{2,1,0:T(4,128)S(1)}, f32[4,3,512,512]{2,3,1,0:T(8,128)S(1)}) fusion(f32[4,3,512,512]{2,3,1,0:T(8,128)} %copy-done, f32[4,3,512]{2,1,0:T(4,128)S(1)} %log_add_fusion, bf16[4,512,1,3,64]{1,0,4,3,2:T(4,128)(2,1)} %copy-done.11, bf16[4,512,3,64]{1,0,3,2:T(4,128)(2,1)} %reshape.218), kind=kOutput, calls=%fused_computation.1 | convolution fusion | flops 412084224 | bytes 26787840 | tf_op jit(solution)/shard_map/bqhd,bkhd->bhqk/dot_general | solution.py:132
  526.0 6.9 multiply_convert_fusion
  541.3 5.1 fusion.21
  552.8 5.6 convolution_bitcast_fusion
  558.4 7.7 %fusion.17 = bf16[4,512,3,64]{1,3,2,0:T(8,128)(2,1)} fusion(f32[4,3,512,512]{2,3,1,0:T(8,128)} %copy-done, f32[4,3,512]{2,1,0:T(4,128)S(1)} %log_add_fusion, bf16[4,512,3,64]{1,0,3,2:T(4,128)(2,1)} %reshape.218), kind=kOutput, calls=%fused_computation.53 | convolution fusion | flops 409337856 | bytes 14180352 | tf_op jit(solution)/shard_map/bhqk,bqhd->bkhd/dot_general | solution.py:133
  575.8 5.8 fusion.75
  585.8 6.2 bitcast_convert_fusion
  601.6 14.3 %all-reduce = f32[2,3,64]{2,1,0:T(4,128)S(1)} all-reduce(f32[2,3,64]{2,1,0:T(4,128)S(1)} %reshape.220), channel_id=10, replica_groups=mesh['dp'=8,'tensor'=4] {'dp'}, use_global_device_ids=true, to_apply=%region_17.18.clone | all-reduce | flops 384 | bytes 3072
  623.8 19.7 %reduce-scatter.20.cloned.1.call-done = f32[96,576]{1,0:T(8,128)} async-done(((f32[768,576]{1,0:T(8,128)}), f32[96,576]{1,0:T(8,128)}) %reduce-scatter.20.cloned.1.call-update) | async-done | bytes 221200
  644.8 67.8 %all-reduce.12.cloned.1.call-done = bf16[2048,768]{1,0:T(8,128)(2,1)} async-done(((bf16[2048,768]{1,0:T(8,128)(2,1)}), bf16[2048,768]{1,0:T(8,128)(2,1)}) %all-reduce.12.cloned.1.call-update) | async-done | bytes 3145744 | tf_op jit(solution)/shard_map/psum | solution.py:152
  712.5 5.4 add_reduce_fusion
  721.0 31.0 %reduce-scatter.26.cloned.1.call-done = f32[96,6]{1,0:T(8,128)} async-done(((f32[768,6]{1,0:T(8,128)}), f32[96,6]{1,0:T(8,128)}) %reduce-scatter.26.cloned.1.call-update) | async-done | bytes 2320
  (212 shorter events, 115.6 us)
Async XLA Ops:
  8.0 49.9 %copy-start.6 = (bf16[4,512,768]{2,1,0:T(8,128)(2,1)S(1)}, bf16[4,512,768]{2,1,0:T(8,128)(2,1)}, u32[]{:S(2)}) copy-start(bf16[4,512,768]{2,1,0:T(8,128)(2,1)} %param.11) | copy-start | bytes 9437188
  8.0 200.9 %all-reduce.6.cloned.1.call-start = ((), (), s32[]{:S(2)}) async-start(), calls=%async_computation.6 | async-start | bytes 6291456 | tf_op jit(solution)/shard_map/psum | solution.py:104
  87.5 128.3 %all-gather.10.cloned.1.call-start = ((), (), s32[]{:S(2)}) async-start(), calls=%async_computation.12 | async-start | bytes 1327104 | tf_op jit(solution)/shard_map/all_gather | solution.py:70
  89.2 134.1 %all-gather.12.cloned.1.call-start = ((), (), s32[]{:S(2)}) async-start(), calls=%async_computation.13 | async-start | bytes 1327104 | tf_op jit(solution)/shard_map/all_gather | solution.py:72
  90.9 258.8 %all-reduce.8.cloned.1.call-start = ((), (), s32[]{:S(2)}) async-start(), calls=%async_computation.7 | async-start | bytes 6291456 | tf_op jit(solution)/shard_map/psum | solution.py:111
  127.3 222.4 %copy-start.22 = (f32[768]{0:T(1024)}, f32[768]{0:T(1024)S(1)}, u32[]{:S(2)}) copy-start(f32[768]{0:T(1024)S(1)} %get-tuple-element.111) | copy-start | bytes 9220
  127.3 222.4 %copy-start.24 = (f32[768]{0:T(1024)}, f32[768]{0:T(1024)S(1)}, u32[]{:S(2)}) copy-start(f32[768]{0:T(1024)S(1)} %get-tuple-element.110) | copy-start | bytes 9220
  229.5 266.2 %all-reduce.10.cloned.1.call-start = ((), (), s32[]{:S(2)}) async-start(), calls=%async_computation.8 | async-start | bytes 6291456 | tf_op jit(solution)/shard_map/psum | solution.py:121
  363.8 7.7 %copy-start.33 = (bf16[1,768,768]{2,1,0:T(8,128)(2,1)S(1)}, bf16[1,768,768]{2,1,0:T(8,128)(2,1)}, u32[]{:S(2)}) copy-start(bf16[1,768,768]{2,1,0:T(8,128)(2,1)} %all-gather.10.cloned.1.call-done) | copy-start | bytes 3538948
  375.5 222.1 %reduce-scatter.24.cloned.1.call-start = ((), (), s32[]{:S(2)}) async-start(), calls=%async_computation.16 | async-start | bytes 73728
  376.3 8.1 %copy-start.17 = (f32[4,3,512]{2,1,0:T(4,128)S(1)}, f32[4,3,512]{2,1,0:T(4,128)}, u32[]{:S(2)}) copy-start(f32[4,3,512]{2,1,0:T(4,128)} %copy-done.16) | copy-start | bytes 73732
  376.4 8.1 %copy-start.19 = (f32[4,3,512]{2,1,0:T(4,128)S(1)}, f32[4,3,512]{2,1,0:T(4,128)}, u32[]{:S(2)}) copy-start(f32[4,3,512]{2,1,0:T(4,128)} %copy-done.18) | copy-start | bytes 73732
  376.4 241.5 %reduce-scatter.18.cloned.1.call-start = ((), (), s32[]{:S(2)}) async-start(), calls=%async_computation.11 | async-start | bytes 2654208 | tf_op jit(solution)/shard_map/reduce_scatter | solution.py:161
  384.4 235.6 %reduce-scatter.16.cloned.1.call-start = ((), (), s32[]{:S(2)}) async-start(), calls=%async_computation.10 | async-start | bytes 2654208 | tf_op jit(solution)/shard_map/reduce_scatter | solution.py:159
  384.5 111.2 %copy-start.23 = (f32[768]{0:T(1024)S(1)}, f32[768]{0:T(1024)}, u32[]{:S(2)}) copy-start(f32[768]{0:T(1024)} %copy-done.22) | copy-start | bytes 9220
  392.5 111.2 %copy-start.21 = (f32[2048]{0:T(1024)S(1)}, f32[2048]{0:T(1024)}, u32[]{:S(2)}) copy-start(f32[2048]{0:T(1024)} %copy-done.20) | copy-start | bytes 24580
  392.6 229.5 %reduce-scatter.22.cloned.1.call-start = ((), (), s32[]{:S(2)}) async-start(), calls=%async_computation.15 | async-start | bytes 884736
  495.7 8.0 %copy-start.5 = (bf16[2048,768]{1,0:T(8,128)(2,1)S(1)}, bf16[2048,768]{1,0:T(8,128)(2,1)}, u32[]{:S(2)}) copy-start(bf16[2048,768]{1,0:T(8,128)(2,1)} %all-reduce.10.cloned.1.call-done) | copy-start | bytes 9437188
  526.0 9.5 %copy-start.13 = (bf16[4,512,1,3,64]{1,0,4,3,2:T(4,128)(2,1)S(1)}, bf16[4,512,1,3,64]{1,0,4,3,2:T(4,128)(2,1)}, u32[]{:S(2)}) copy-start(bf16[4,512,1,3,64]{1,0,4,3,2:T(4,128)(2,1)} %copy-done.12) | copy-start | bytes 2359300
  566.2 77.4 %reduce-scatter.20.cloned.1.call-start = ((), (), s32[]{:S(2)}) async-start(), calls=%async_computation.14 | async-start | bytes 2211840
  584.5 128.0 %all-reduce.12.cloned.1.call-start = ((), (), s32[]{:S(2)}) async-start(), calls=%async_computation.9 | async-start | bytes 6291456 | tf_op jit(solution)/shard_map/psum | solution.py:152
  585.8 8.3 %copy-start.27 = (f32[768]{0:T(1024)S(1)}, f32[768]{0:T(1024)}, u32[]{:S(2)}) copy-start(f32[768]{0:T(1024)} %convert_reduce_fusion) | copy-start | bytes 9220
  585.8 11.7 %copy-start.25 = (f32[768]{0:T(1024)S(1)}, f32[768]{0:T(1024)}, u32[]{:S(2)}) copy-start(f32[768]{0:T(1024)} %get-tuple-element.104) | copy-start | bytes 9220
  585.8 15.2 %copy-start.26 = (f32[768]{0:T(1024)S(1)}, f32[768]{0:T(1024)}, u32[]{:S(2)}) copy-start(f32[768]{0:T(1024)} %get-tuple-element.107) | copy-start | bytes 9220
  592.1 9.0 %copy-start.10 = (bf16[2048,3,192]{0,2,1:T(8,128)(2,1)S(1)}, bf16[2048,3,192]{0,2,1:T(8,128)(2,1)}, u32[]{:S(2)}) copy-start(bf16[2048,3,192]{0,2,1:T(8,128)(2,1)} %constant_dynamic-update-slice_fusion) | copy-start | bytes 7077892
  592.1 31.0 %copy-start.15 = (f32[3,192,96]{2,1,0:T(8,128)S(1)}, f32[3,192,96]{2,1,0:T(8,128)}, u32[]{:S(2)}) copy-start(f32[3,192,96]{2,1,0:T(8,128)} %param.17) | copy-start | bytes 663556
  592.1 159.8 %reduce-scatter.26.cloned.1.call-start = ((), (), s32[]{:S(2)}) async-start(), calls=%async_computation.17 | async-start | bytes 442368
  598.4 119.6 %copy-start.28 = (f32[6,16]{1,0:T(8,128)}, f32[6,16]{1,0:T(8,128)S(1)}, u32[]{:S(2)}) copy-start(f32[6,16]{1,0:T(8,128)S(1)} %copy.176) | copy-start | bytes 1156
  616.6 101.3 %copy-start.30 = (f32[2,3,8]{2,0,1:T(2,128)}, f32[2,3,8]{2,0,1:T(2,128)S(1)}, u32[]{:S(2)}) copy-start(f32[2,3,8]{2,0,1:T(2,128)S(1)} %get-tuple-element.115) | copy-start | bytes 580
  623.1 94.8 %copy-start.14 = (f32[192,96]{1,0:T(8,128)}, f32[192,96]{1,0:T(8,128)S(1)}, u32[]{:S(2)}) copy-start(f32[192,96]{1,0:T(8,128)S(1)} %copy.174) | copy-start | bytes 221188
  644.7 73.2 %copy-start.31 = (f32[1,768]{1,0:T(1,128)S(1)}, f32[1,768]{1,0:T(1,128)}, u32[]{:S(2)}) copy-start(f32[1,768]{1,0:T(1,128)} %reshape.225) | copy-start | bytes 9220
  644.7 108.1 %copy-start.32 = (f32[3,6,96]{2,1,0:T(8,128)S(1)}, f32[3,6,96]{2,1,0:T(8,128)}, u32[]{:S(2)}) copy-start(f32[3,6,96]{2,1,0:T(8,128)} %param.21) | copy-start | bytes 20740
  (19 other events, 79.1 us)
Sparse Core Ops, SparseCore 0:
  87.6 121.2 all-reduce.5
  229.6 120.0 all-reduce.7
  375.6 120.0 all-reduce.9
  592.2 120.2 all-reduce.11
Sparse Core Ops, SparseCore 1:
  90.4 25.2 all-gather.9
  118.0 23.8 all-gather.11
  379.6 32.5 reduce-scatter.23
  416.1 42.2 reduce-scatter.17
  462.2 42.2 reduce-scatter.15
  566.2 33.9 reduce-scatter.21
  603.5 40.0 reduce-scatter.19
  719.0 32.9 reduce-scatter.25
where the time goes:
time: 772 us; the launch traced here: 761 us
  waiting for transfers between devices  423 us (55%)
  matrix products  94.3 us (12%)
  local copies, waits for them, and re-layouts  90.2 us (12%)
  blocking collectives  71.4 us (9%)
  other arithmetic  63 us (8%)
  between operations  17.6 us (2%)
    psum x1, waiting for transfers between devices, body(): ffn = lax.psum(ffn_part.astype(jnp.bfloat16), 'tensor').astype(jnp.float32)  120 us
    psum x1, waiting for transfers between devices, body(): lax.psum(feed_part.astype(jnp.bfloat16), 'tensor').astype(jnp.float32)  103 us
    psum x1, waiting for transfers between devices, body(): lax.psum(attn_part.astype(jnp.bfloat16), 'tensor').astype(jnp.float32)  81.6 us
    psum x1, waiting for transfers between devices, body(): lax.psum(input_part.astype(jnp.bfloat16), 'tensor').astype(jnp.float32)  67.8 us
    unnamed x16, waiting for transfers between devices  50.9 us
    unnamed x98, local copies, waits for them, and re-layouts  29.5 us
    reduce_sum x4, other arithmetic, layer_norm(): center = value - jnp.mean(value, axis=-1, keepdims=True)  18.3 us
    dot_general x2, matrix products, contract_rows(): lax.dot_general(left, right, (((0,), (0,)), ((), ())), preferred_element_...  16 us
  transfers between devices with their start and end apart: 12, of which 6 were waited for; matrix products, arithmetic and copies ran while one was open for 21% of the time, Pallas kernels for 0%

commit v1 on v0

--- a/solution.py
+++ b/solution.py
@@ -108,7 +108,9 @@
     act, gelu_pull = jax.vjp(gelu_exact, up)
     act_b = act.astype(bf)
     ffn_part = jnp.dot(act_b, w_down, preferred_element_type=fl)
-    ffn = lax.psum(ffn_part.astype(jnp.bfloat16), "tensor").astype(jnp.float32)
+    ffn = jnp.sum(lax.all_gather(ffn_part.astype(jnp.bfloat16), "tensor"), axis=0).astype(
+        jnp.float32
+    )
     out, second_pull = jax.vjp(layer_norm, first + ffn + vec[5], vec[2], vec[3])
     grad_r2, grad_g2, grad_b2 = second_pull(cotangent.astype(fl))
     grad_ffn = grad_r2.astype(bf)

time: 772 us -> 877 us (1.14)
  waiting for transfers between devices: 423 us -> 519 us
    all_gather x0 -> x1, waiting for transfers between devices: none -> 217 us  [body(): lax.all_gather(ffn_part.astype(jnp.bfloat16), 'tensor')]
    psum x1 -> x0, waiting for transfers between devices: 120 us -> none  [body(): ffn = lax.psum(ffn_part.astype(jnp.bfloat16), 'tensor').astype(jnp.float32)]
  transfers between devices with their start and end apart: 12 -> 12, of which waited for: 6 -> 6; matrix products, arithmetic and copies ran while one was open for 21% -> 19% of each run, Pallas kernels for 0% -> 0%
where the time goes in v1:
time: 877 us; the launch traced here: 865 us
  waiting for transfers between devices  519 us (59%)
  matrix products  94.8 us (11%)
  local copies, waits for them, and re-layouts  90 us (10%)
  blocking collectives  70.9 us (8%)
  other arithmetic  70.8 us (8%)
  between operations  17.9 us (2%)
    all_gather x1, waiting for transfers between devices, body(): lax.all_gather(ffn_part.astype(jnp.bfloat16), 'tensor')  217 us
    psum x1, waiting for transfers between devices, body(): lax.psum(feed_part.astype(jnp.bfloat16), 'tensor').astype(jnp.float32)  102 us
    psum x1, waiting for transfers between devices, body(): lax.psum(attn_part.astype(jnp.bfloat16), 'tensor').astype(jnp.float32)  82 us
    psum x1, waiting for transfers between devices, body(): lax.psum(input_part.astype(jnp.bfloat16), 'tensor').astype(jnp.float32)  67.9 us
    unnamed x16, waiting for transfers between devices  50.8 us
    unnamed x98, local copies, waits for them, and re-layouts  29.4 us
  transfers between devices with their start and end apart: 12, of which 6 were waited for; matrix products, arithmetic and copies ran while one was open for 19% of the time, Pallas kernels for 0%

profile of v1, /device:TPU:0, one launch (start us, length us, event | category | flops | bytes accessed | tf_op | source)
XLA Modules:
  0.0 864.9 jit_solution(9425358926136026017)
XLA Ops:
  9.0 10.6 %all-gather.1 = bf16[1,2,3,64]{2,1,0,3:T(2,128)(2,1)S(1)} all-gather(bf16[1,2,3,8]{2,1,0,3:T(2,128)(2,1)S(1)} %copy.181), channel_id=3, replica_groups=mesh['dp'=8,'tensor'=4] {'dp'}, dimensions={3}, use_global_device_ids=true | all-gather | bytes 864 | tf_op jit(solution)/shard_map/all_gather | solution.py:68
  22.8 11.3 %all-gather.2 = bf16[1,192,768]{1,0,2:T(2,128)(2,1)} all-gather(bf16[1,192,96]{1,0,2:T(2,128)(2,1)S(1)} %copy.142), channel_id=4, replica_groups=mesh['dp'=8,'tensor'=4] {'dp'}, dimensions={2}, use_global_device_ids=true | all-gather | bytes 331776 | tf_op jit(solution)/shard_map/all_gather | solution.py:69
  38.6 15.8 %all-gather = bf16[1,768,3,192]{3,2,0,1:T(4,128)(2,1)} all-gather(bf16[1,96,3,192]{3,2,0,1:T(4,128)(2,1)} %copy.132), channel_id=2, replica_groups=mesh['dp'=8,'tensor'=4] {'dp'}, dimensions={1}, use_global_device_ids=true | all-gather | bytes 995328 | tf_op jit(solution)/shard_map/all_gather | solution.py:67
  62.9 6.2 reshape.215
  71.5 4.4 fusion.73
  93.1 8.7 %all-gather.5 = bf16[1,6,128]{1,0,2:T(2,128)(2,1)S(1)} all-gather(bf16[1,6,16]{1,0,2:T(2,128)(2,1)} %copy.145), channel_id=7, replica_groups=mesh['dp'=8,'tensor'=4] {'dp'}, dimensions={2}, use_global_device_ids=true | all-gather | bytes 1728 | tf_op jit(solution)/shard_map/all_gather | solution.py:71
  103.2 10.3 %all-gather.3 = bf16[1,6,768]{1,0,2:T(2,128)(2,1)S(1)} all-gather(bf16[1,6,96]{1,0,2:T(2,128)(2,1)S(1)} %copy.185), channel_id=5, replica_groups=mesh['dp'=8,'tensor'=4] {'dp'}, dimensions={2}, use_global_device_ids=true | all-gather | bytes 10368 | tf_op jit(solution)/shard_map/all_gather | solution.py:73
  113.9 13.0 %slice_reduce_fusion.1 = (f32[768]{0:T(1024)S(1)}, f32[768]{0:T(1024)S(1)}, f32[768]{0:T(1024)S(1)}, f32[768]{0:T(1024)S(1)}, f32[768]{0:T(1024)S(1)}, /*index=5*/f32[768]{0:T(1024)S(1)}) fusion(f32[1,6,768]{1,0,2:T(1,128)S(1)} %convert_element_type.171), kind=kLoop, calls=%fused_computation.78 | loop fusion | bytes 36864 | tf_op jit(solution)/shard_map/slice | solution.py:114
  126.9 82.0 %all-reduce.5.cloned.1.call-done = bf16[2048,768]{1,0:T(8,128)(2,1)} async-done(((bf16[2048,768]{1,0:T(8,128)(2,1)}), bf16[2048,768]{1,0:T(8,128)(2,1)}) %all-reduce.5.cloned.1.call-update) | async-done | bytes 3145744 | tf_op jit(solution)/shard_map/psum | solution.py:104
  215.9 7.4 multiply_convert_fusion.1
  223.3 6.2 convolution_convert_fusion.1
  230.0 216.9 %all-gather.16.cloned.1.call-done = bf16[8192,768]{1,0:T(8,128)(2,1)} async-done(((bf16[2048,768]{1,0:T(8,128)(2,1)}), bf16[8192,768]{1,0:T(8,128)(2,1)}) %all-gather.16.cloned.1.call-update) | async-done | bytes 12582928 | tf_op jit(solution)/shard_map/all_gather | solution.py:111
  446.9 8.6 reduce_sum.176
  464.3 4.3 fusion.66
  468.7 5.9 convert_reduce_fusion.1
  481.2 8.5 fusion.60
  489.8 8.0 fusion.61
  498.1 101.6 %all-reduce.7.cloned.1.call-done = bf16[2048,768]{1,0:T(8,128)(2,1)} async-done(((bf16[2048,768]{1,0:T(8,128)(2,1)}), bf16[2048,768]{1,0:T(8,128)(2,1)}) %all-reduce.7.cloned.1.call-update) | async-done | bytes 3145744 | tf_op jit(solution)/shard_map/psum | solution.py:123
  599.7 8.0 multiply_reduce_fusion.1
  607.7 6.1 fusion.65
  621.6 8.3 multiply_reduce_fusion
  629.9 6.9 multiply_convert_fusion
  645.1 5.1 fusion.21
  656.5 5.6 convolution_bitcast_fusion
  662.2 7.8 fusion.17
  679.7 5.8 fusion.75
  689.7 6.2 bitcast_convert_fusion
  705.5 14.3 %all-reduce = f32[2,3,64]{2,1,0:T(4,128)S(1)} all-reduce(f32[2,3,64]{2,1,0:T(4,128)S(1)} %reshape.220), channel_id=11, replica_groups=mesh['dp'=8,'tensor'=4] {'dp'}, use_global_device_ids=true, to_apply=%region_17.18.clone | all-reduce | flops 384 | bytes 3072
  727.7 19.6 %reduce-scatter.20.cloned.1.call-done = f32[96,576]{1,0:T(8,128)} async-done(((f32[768,576]{1,0:T(8,128)}), f32[96,576]{1,0:T(8,128)}) %reduce-scatter.20.cloned.1.call-update) | async-done | bytes 221200
  748.6 67.9 %all-reduce.9.cloned.1.call-done = bf16[2048,768]{1,0:T(8,128)(2,1)} async-done(((bf16[2048,768]{1,0:T(8,128)(2,1)}), bf16[2048,768]{1,0:T(8,128)(2,1)}) %all-reduce.9.cloned.1.call-update) | async-done | bytes 3145744 | tf_op jit(solution)/shard_map/psum | solution.py:154
  816.4 5.4 add_reduce_fusion
  824.9 31.0 %reduce-scatter.26.cloned.1.call-done = f32[96,6]{1,0:T(8,128)} async-done(((f32[768,6]{1,0:T(8,128)}), f32[96,6]{1,0:T(8,128)}) %reduce-scatter.26.cloned.1.call-update) | async-done | bytes 2320
  (213 shorter events, 119.6 us)
Async XLA Ops:
  8.0 49.9 %copy-start.6 = (bf16[4,512,768]{2,1,0:T(8,128)(2,1)S(1)}, bf16[4,512,768]{2,1,0:T(8,128)(2,1)}, u32[]{:S(2)}) copy-start(bf16[4,512,768]{2,1,0:T(8,128)(2,1)} %param.11) | copy-start | bytes 9437188
  8.0 200.9 %all-reduce.5.cloned.1.call-start = ((), (), s32[]{:S(2)}) async-start(), calls=%async_computation.6 | async-start | bytes 6291456 | tf_op jit(solution)/shard_map/psum | solution.py:104
  87.5 128.4 %all-gather.12.cloned.1.call-start = ((), (), s32[]{:S(2)}) async-start(), calls=%async_computation.11 | async-start | bytes 1327104 | tf_op jit(solution)/shard_map/all_gather | solution.py:70
  89.2 134.2 %all-gather.14.cloned.1.call-start = ((), (), s32[]{:S(2)}) async-start(), calls=%async_computation.12 | async-start | bytes 1327104 | tf_op jit(solution)/shard_map/all_gather | solution.py:72
  90.9 356.0 %all-gather.16.cloned.1.call-start = ((), (), s32[]{:S(2)}) async-start(), calls=%async_computation.13 | async-start | bytes 15728640 | tf_op jit(solution)/shard_map/all_gather | solution.py:111
  126.9 328.6 %copy-start.22 = (f32[768]{0:T(1024)}, f32[768]{0:T(1024)S(1)}, u32[]{:S(2)}) copy-start(f32[768]{0:T(1024)S(1)} %get-tuple-element.111) | copy-start | bytes 9220
  126.9 328.6 %copy-start.24 = (f32[768]{0:T(1024)}, f32[768]{0:T(1024)S(1)}, u32[]{:S(2)}) copy-start(f32[768]{0:T(1024)S(1)} %get-tuple-element.110) | copy-start | bytes 9220
  229.6 370.2 %all-reduce.7.cloned.1.call-start = ((), (), s32[]{:S(2)}) async-start(), calls=%async_computation.7 | async-start | bytes 6291456 | tf_op jit(solution)/shard_map/psum | solution.py:123
  468.7 7.6 copy-start.33
  480.3 221.2 %reduce-scatter.24.cloned.1.call-start = ((), (), s32[]{:S(2)}) async-start(), calls=%async_computation.16 | async-start | bytes 73728
  481.1 8.6 copy-start.17
  481.1 8.6 copy-start.19
  481.2 240.6 %reduce-scatter.18.cloned.1.call-start = ((), (), s32[]{:S(2)}) async-start(), calls=%async_computation.10 | async-start | bytes 2654208 | tf_op jit(solution)/shard_map/reduce_scatter | solution.py:163
  489.7 234.2 %reduce-scatter.16.cloned.1.call-start = ((), (), s32[]{:S(2)}) async-start(), calls=%async_computation.9 | async-start | bytes 2654208 | tf_op jit(solution)/shard_map/reduce_scatter | solution.py:161
  489.8 109.9 %copy-start.23 = (f32[768]{0:T(1024)S(1)}, f32[768]{0:T(1024)}, u32[]{:S(2)}) copy-start(f32[768]{0:T(1024)} %copy-done.22) | copy-start | bytes 9220
  497.9 109.8 %copy-start.21 = (f32[2048]{0:T(1024)S(1)}, f32[2048]{0:T(1024)}, u32[]{:S(2)}) copy-start(f32[2048]{0:T(1024)} %copy-done.20) | copy-start | bytes 24580
  497.9 228.1 %reduce-scatter.22.cloned.1.call-start = ((), (), s32[]{:S(2)}) async-start(), calls=%async_computation.15 | async-start | bytes 884736
  599.7 8.0 copy-start.5
  629.9 9.5 %copy-start.13 = (bf16[4,512,1,3,64]{1,0,4,3,2:T(4,128)(2,1)S(1)}, bf16[4,512,1,3,64]{1,0,4,3,2:T(4,128)(2,1)}, u32[]{:S(2)}) copy-start(bf16[4,512,1,3,64]{1,0,4,3,2:T(4,128)(2,1)} %copy-done.12) | copy-start | bytes 2359300
  669.9 77.4 %reduce-scatter.20.cloned.1.call-start = ((), (), s32[]{:S(2)}) async-start(), calls=%async_computation.14 | async-start | bytes 2211840
  688.3 128.1 %all-reduce.9.cloned.1.call-start = ((), (), s32[]{:S(2)}) async-start(), calls=%async_computation.8 | async-start | bytes 6291456 | tf_op jit(solution)/shard_map/psum | solution.py:154
  689.7 8.3 copy-start.27
  689.7 11.7 %copy-start.25 = (f32[768]{0:T(1024)S(1)}, f32[768]{0:T(1024)}, u32[]{:S(2)}) copy-start(f32[768]{0:T(1024)} %get-tuple-element.104) | copy-start | bytes 9220
  689.7 15.2 %copy-start.26 = (f32[768]{0:T(1024)S(1)}, f32[768]{0:T(1024)}, u32[]{:S(2)}) copy-start(f32[768]{0:T(1024)} %get-tuple-element.107) | copy-start | bytes 9220
  696.0 9.0 %copy-start.10 = (bf16[2048,3,192]{0,2,1:T(8,128)(2,1)S(1)}, bf16[2048,3,192]{0,2,1:T(8,128)(2,1)}, u32[]{:S(2)}) copy-start(bf16[2048,3,192]{0,2,1:T(8,128)(2,1)} %constant_dynamic-update-slice_fusion) | copy-start | bytes 7077892
  696.0 31.0 %copy-start.15 = (f32[3,192,96]{2,1,0:T(8,128)S(1)}, f32[3,192,96]{2,1,0:T(8,128)}, u32[]{:S(2)}) copy-start(f32[3,192,96]{2,1,0:T(8,128)} %param.17) | copy-start | bytes 663556
  696.0 159.9 %reduce-scatter.26.cloned.1.call-start = ((), (), s32[]{:S(2)}) async-start(), calls=%async_computation.17 | async-start | bytes 442368
  702.3 119.6 %copy-start.28 = (f32[6,16]{1,0:T(8,128)}, f32[6,16]{1,0:T(8,128)S(1)}, u32[]{:S(2)}) copy-start(f32[6,16]{1,0:T(8,128)S(1)} %copy.176) | copy-start | bytes 1156
  720.5 101.3 %copy-start.30 = (f32[2,3,8]{2,0,1:T(2,128)}, f32[2,3,8]{2,0,1:T(2,128)S(1)}, u32[]{:S(2)}) copy-start(f32[2,3,8]{2,0,1:T(2,128)S(1)} %get-tuple-element.115) | copy-start | bytes 580
  727.0 94.9 %copy-start.14 = (f32[192,96]{1,0:T(8,128)}, f32[192,96]{1,0:T(8,128)S(1)}, u32[]{:S(2)}) copy-start(f32[192,96]{1,0:T(8,128)S(1)} %copy.174) | copy-start | bytes 221188
  748.5 73.3 %copy-start.31 = (f32[1,768]{1,0:T(1,128)S(1)}, f32[1,768]{1,0:T(1,128)}, u32[]{:S(2)}) copy-start(f32[1,768]{1,0:T(1,128)} %reshape.225) | copy-start | bytes 9220
  748.6 108.2 %copy-start.32 = (f32[3,6,96]{2,1,0:T(8,128)S(1)}, f32[3,6,96]{2,1,0:T(8,128)}, u32[]{:S(2)}) copy-start(f32[3,6,96]{2,1,0:T(8,128)} %param.21) | copy-start | bytes 20740
  (19 other events, 79.0 us)
Sparse Core Ops, SparseCore 0:
  87.6 121.2 all-reduce.4
  229.7 217.1 all-gather.15
  480.4 119.2 all-reduce.6
  696.1 120.2 all-reduce.8
Sparse Core Ops, SparseCore 1:
  90.4 25.2 all-gather.11
  117.9 23.8 all-gather.13
  484.4 31.7 reduce-scatter.23
  520.1 42.2 reduce-scatter.17
  566.2 42.2 reduce-scatter.15
  670.0 33.9 reduce-scatter.21
  707.2 40.0 reduce-scatter.19
  822.9 32.9 reduce-scatter.25
